TPU v7x, 32 devices: a whole 2x2x4 slice. The times are simulated.
32 devices in a mesh: fsdp: 8 (over z, y), dp: 4 (over x, core).
Axes of the slice: x: 2, y: 2, z: 4, core: 2. Of those that a mesh axis runs over, the one named last changes fastest.
Arguments:
- hidden_in: bfloat16 [128, 128, 768], P(('fsdp', 'dp')), may hold values from -6 to 6
- query_key_value_weight: bfloat16 [768, 2304], P('fsdp'), may hold values from -0.21875 to 0.21875
- attention_output_weight: bfloat16 [768, 768], P('fsdp'), may hold values from -0.625 to 0.625
- gate_up_weight: bfloat16 [768, 6144], P('fsdp'), may hold values from -0.21875 to 0.21875
- down_weight: bfloat16 [3072, 768], P('fsdp'), may hold values from -0.109375 to 0.109375
- gain_attn: bfloat16 [768], P('fsdp'), may hold values from 0.25 to 1.75
- shift_attn: bfloat16 [768], P('fsdp'), may hold values from -3 to 3
- gain_ffn: bfloat16 [768], P('fsdp'), may hold values from 0.25 to 1.75
- shift_ffn: bfloat16 [768], P('fsdp'), may hold values from -3 to 3
- masked_output_gradient: bfloat16 [128, 32, 768], P(('fsdp', 'dp')), may hold values from -6 to 6
- positions: int32 [128, 32], P(('fsdp', 'dp')), may hold values from 0 to 127, as said below
- mask_counts: int32 [128], P(('fsdp', 'dp')), may hold values from 8 to 32
Outputs:
- layer_out: bfloat16 [128, 128, 768], P(('fsdp', 'dp'))
- grad_in: float32 [128, 128, 768], P(('fsdp', 'dp'))
- grad_qkv: float32 [768, 2304], P('fsdp')
- grad_out_proj: float32 [768, 768], P('fsdp')
- grad_up: float32 [768, 6144], P('fsdp')
- grad_down: float32 [3072, 768], P('fsdp')
- grad_gain_attn: float32 [768], P('fsdp')
- grad_shift_attn: float32 [768], P('fsdp')
- grad_gain_ffn: float32 [768], P('fsdp')
- grad_shift_ffn: float32 [768], P('fsdp')
Inputs may be any that keep to these rules, and one draw needn't show every extreme that they name: Within one sequence the listed positions are distinct.
All inputs are finite; a program needn't handle non-finite values.
Results may differ from a plain program's by a relative error of at most 0.015.
Values may be sent and summed in bfloat16 or wider, within the bound.
No kernel may reach another device: no remote copies, remote signals or barrier semaphores. Data moves between devices by JAX's collectives and lax.ppermute only.
A program may use at most 192 MiB of HBM per device.

v0:
```python
import jax
import jax.numpy as jnp
from jax import lax
from jax.sharding import PartitionSpec as P

HEADS = 12
HEAD_DIM = 64
FF = 3072
EPS = 1e-12
F32 = jnp.float32
LOW = jnp.bfloat16
AXES = ("fsdp", "dp")


def mm(a, b):
    return jnp.dot(a, b, preferred_element_type=F32)


def slopes():
    return jnp.exp2(-8.0 * (jnp.arange(HEADS, dtype=F32) + 1.0) / HEADS)


def norm_parts(value):
    center = value - jnp.mean(value, axis=-1, keepdims=True)
    rstd = lax.rsqrt(jnp.mean(center * center, axis=-1, keepdims=True) + EPS)
    return (center * rstd, rstd)


def norm_back(grad, unit, rstd, gain):
    scaled = grad * gain
    return rstd * (
        scaled
        - jnp.mean(scaled, axis=-1, keepdims=True)
        - unit * jnp.mean(scaled * unit, axis=-1, keepdims=True)
    )


def pick(onehot, rows):
    if rows.dtype == LOW:
        return jnp.einsum(
            "svj,sjd->svd", onehot.astype(LOW), rows, preferred_element_type=F32
        ).astype(LOW)
    return jnp.einsum("svj,sjd->svd", onehot, rows, precision=lax.Precision.HIGHEST)


def gather_weights(w_qkv, w_out, w_up, w_down):
    fsdp = lax.axis_size("fsdp")
    dp = lax.axis_size("dp")
    rows, width = w_out.shape
    if rows % (8 * dp):
        return (
            lax.all_gather(w_qkv, "fsdp", axis=0, tiled=True),
            lax.all_gather(w_out, "fsdp", axis=0, tiled=True),
            lax.all_gather(w_up, "fsdp", axis=0, tiled=True),
            lax.all_gather(w_down, "fsdp", axis=0, tiled=True),
        )
    mine = lax.axis_index("dp")
    part = rows // dp
    group = w_down.shape[0] // rows
    joined = jnp.concatenate([w_qkv, w_out, w_up], axis=1)
    joined = lax.dynamic_slice_in_dim(joined, mine * part, part, axis=0)
    down = lax.dynamic_slice_in_dim(w_down, mine * part * group, part * group, axis=0)
    down = jnp.concatenate([down[k * part : (k + 1) * part] for k in range(group)], axis=1)
    full = lax.all_gather(jnp.concatenate([joined, down], axis=1), AXES, axis=0, tiled=True)
    a, b = (w_qkv.shape[1], w_qkv.shape[1] + w_out.shape[1])
    c = b + w_up.shape[1]
    full_down = full[:, c:].reshape(fsdp * dp, part, group, width)
    full_down = full_down.transpose(0, 2, 1, 3).reshape(fsdp * dp * part * group, width)
    return (full[:, :a], full[:, a:b], full[:, b:c], full_down)


def scatter_grads(g_qkv, g_out, g_up, g_down):
    fsdp = lax.axis_size("fsdp")
    dp = lax.axis_size("dp")
    width = g_out.shape[1]
    rows = g_out.shape[0] // fsdp
    if rows % (8 * dp):
        return tuple(
            (
                lax.psum(lax.psum_scatter(g, "fsdp", scatter_dimension=0, tiled=True), "dp")
                for g in (g_qkv, g_out, g_up, g_down)
            )
        )
    part = rows // dp
    group = g_down.shape[0] // g_out.shape[0]
    down = g_down.reshape(fsdp * dp, group, part, width).transpose(0, 2, 1, 3)
    down = down.reshape(fsdp * rows, group * width)
    joined = jnp.concatenate([g_qkv, g_out, g_up, down], axis=1).astype(LOW)
    mine = lax.psum_scatter(joined, AXES, scatter_dimension=0, tiled=True)
    full = lax.all_gather(mine, "dp", axis=0, tiled=True).astype(F32)
    a, b = (g_qkv.shape[1], g_qkv.shape[1] + width)
    c = b + g_up.shape[1]
    full_down = full[:, c:].reshape(dp, part, group, width).transpose(0, 2, 1, 3)
    return (full[:, :a], full[:, a:b], full[:, b:c], full_down.reshape(rows * group, width))


def on_device(
    hidden_in,
    w_qkv,
    w_out,
    w_up,
    w_down,
    gain_attn,
    shift_attn,
    gain_ffn,
    shift_ffn,
    grad_listed,
    positions,
    counts,
):
    seqs, length, width = hidden_in.shape
    tokens = seqs * length
    most = positions.shape[1]
    norms = jnp.stack([gain_attn, shift_attn, gain_ffn, shift_ffn])
    norms = lax.all_gather(norms, "fsdp", axis=1, tiled=True).astype(F32)
    w_qkv, w_out, w_up, w_down = gather_weights(w_qkv, w_out, w_up, w_down)
    live = jnp.arange(most, dtype=jnp.int32)[None, :] < counts[:, None]
    onehot = (positions[:, :, None] == jnp.arange(length, dtype=jnp.int32)).astype(F32)
    rows_in = hidden_in.reshape(tokens, width)
    slope = slopes()
    scale = HEAD_DIM ** (-0.5)
    qkv = mm(rows_in, w_qkv).astype(LOW)
    split = qkv.reshape(seqs, length, 3, HEADS, HEAD_DIM)
    q, k, v = (split[:, :, 0], split[:, :, 1], split[:, :, 2])
    place = jnp.arange(length, dtype=F32)
    bias = -slope[:, None, None] * jnp.abs(place[:, None] - place[None, :])
    s = jnp.einsum("sqhc,skhc->shqk", q, k, preferred_element_type=F32) * scale + bias
    p = jax.nn.softmax(s, axis=-1).astype(LOW)
    att = jnp.einsum("shqk,skhc->sqhc", p, v, preferred_element_type=F32).astype(LOW)
    att = att.reshape(tokens, width)
    r1 = rows_in.astype(F32) + mm(att, w_out)
    unit1, _ = norm_parts(r1)
    h1 = unit1 * norms[0] + norms[1]
    h1_low = h1.astype(LOW)
    u = mm(h1_low, w_up)
    act = (jax.nn.gelu(u[:, :FF], approximate=False) * u[:, FF:]).astype(LOW)
    r2 = h1 + mm(act, w_down)
    unit2, _ = norm_parts(r2)
    layer_out = (unit2 * norms[2] + norms[3]).astype(LOW).reshape(seqs, length, width)

    def listed(a):
        return pick(onehot, a.reshape(seqs, length, -1)).reshape(seqs * most, -1)

    dy = jnp.where(live[:, :, None], grad_listed, 0).astype(F32).reshape(seqs * most, width)
    unit2_m, rstd2_m = norm_parts(listed(r2))
    g_gain_ffn = jnp.sum(dy * unit2_m, axis=0)
    g_shift_ffn = jnp.sum(dy, axis=0)
    dr2 = norm_back(dy, unit2_m, rstd2_m, norms[2])
    e2 = dr2.astype(LOW)
    h1_m = listed(h1_low)
    u_m = mm(h1_m, w_up)
    gate, up = (u_m[:, :FF], u_m[:, FF:])
    cdf = 0.5 * (1.0 + lax.erf(gate * 0.5**0.5))
    pdf = jnp.exp(-0.5 * gate * gate) * (2.0 * jnp.pi) ** (-0.5)
    gelu = gate * cdf
    act_m = (gelu * up).astype(LOW)
    g_down = jnp.einsum("nf,nd->fd", act_m, e2, preferred_element_type=F32)
    dact = jnp.einsum("nd,fd->nf", e2, w_down, preferred_element_type=F32)
    du = jnp.concatenate([dact * up * (cdf + gate * pdf), dact * gelu], axis=1).astype(LOW)
    g_up = jnp.einsum("nd,nf->df", h1_m, du, preferred_element_type=F32)
    dh1 = dr2 + jnp.einsum("nf,df->nd", du, w_up, preferred_element_type=F32)
    unit1_m, rstd1_m = norm_parts(listed(r1))
    g_gain_attn = jnp.sum(dh1 * unit1_m, axis=0)
    g_shift_attn = jnp.sum(dh1, axis=0)
    dr1 = norm_back(dh1, unit1_m, rstd1_m, norms[0])
    e1 = dr1.astype(LOW)
    g_out = jnp.einsum("nd,ne->de", listed(att), e1, preferred_element_type=F32)
    datt = jnp.einsum("ne,de->nd", e1, w_out, preferred_element_type=F32).astype(LOW)
    datt = datt.reshape(seqs, most, HEADS, HEAD_DIM)
    q_m = listed(qkv[:, :width]).reshape(seqs, most, HEADS, HEAD_DIM)
    away = jnp.abs(positions[:, :, None].astype(F32) - place[None, None, :])
    s_m = jnp.einsum("sqhc,skhc->shqk", q_m, k, preferred_element_type=F32) * scale
    p_m = jax.nn.softmax(s_m - slope[None, :, None, None] * away[:, None], axis=-1)
    dv = jnp.einsum("shqk,sqhc->skhc", p_m.astype(LOW), datt, preferred_element_type=F32)
    dp = jnp.einsum("sqhc,skhc->shqk", datt, v, preferred_element_type=F32)
    ds = (p_m * (dp - jnp.sum(dp * p_m, axis=-1, keepdims=True))).astype(LOW)
    dq_m = (jnp.einsum("shqk,skhc->sqhc", ds, k, preferred_element_type=F32) * scale).astype(LOW)
    dk = (jnp.einsum("shqk,sqhc->skhc", ds, q_m, preferred_element_type=F32) * scale).astype(LOW)
    put = (onehot * live[:, :, None]).astype(LOW)
    dq = jnp.einsum(
        "svj,svd->sjd", put, dq_m.reshape(seqs, most, width), preferred_element_type=F32
    )
    dqkv = jnp.concatenate(
        [
            dq.astype(LOW).reshape(tokens, width),
            dk.reshape(tokens, width),
            dv.astype(LOW).reshape(tokens, width),
        ],
        axis=1,
    )
    g_qkv = jnp.einsum("nd,ne->de", rows_in, dqkv, preferred_element_type=F32)
    dr1_all = jnp.einsum(
        "svj,svd->sjd",
        onehot * live[:, :, None],
        dr1.reshape(seqs, most, width),
        precision=lax.Precision.HIGHEST,
    )
    grad_in = dr1_all.reshape(tokens, width) + jnp.einsum(
        "ne,de->nd", dqkv, w_qkv, preferred_element_type=F32
    )
    owned = scatter_grads(g_qkv, g_out, g_up, g_down)
    small = lax.psum(jnp.stack([g_gain_attn, g_shift_attn, g_gain_ffn, g_shift_ffn]), AXES)
    share = width // lax.axis_size("fsdp")
    small = lax.dynamic_slice_in_dim(small, lax.axis_index("fsdp") * share, share, axis=1)
    return (
        layer_out,
        grad_in.reshape(seqs, length, width),
        *owned,
        small[0],
        small[1],
        small[2],
        small[3],
    )


def solution(mesh):
    rows3 = P(("fsdp", "dp"), None, None)
    rows2 = P("fsdp", None)
    rows1 = P("fsdp")
    return jax.shard_map(
        on_device,
        mesh=mesh,
        in_specs=(
            rows3,
            rows2,
            rows2,
            rows2,
            rows2,
            rows1,
            rows1,
            rows1,
            rows1,
            rows3,
            P(("fsdp", "dp"), None),
            P(("fsdp", "dp")),
        ),
        out_specs=(rows3, rows3, rows2, rows2, rows2, rows2, rows1, rows1, rows1, rows1),
        check_vma=False,
    )
```

profile of v0, /device:TPU:0, one launch (start us, length us, event | category | flops | bytes accessed | tf_op | source)
XLA Modules:
  0.0 575.9 jit_solution(14297018178041532854)
XLA Ops:
  13.0 22.6 %all-gather = bf16[8,96,4]{1,2,0:T(4,128)(2,1)S(1)} all-gather(bf16[1,96,4]{1,2,0:T(4,128)(2,1)S(1)} %maximum_bitcast_fusion), channel_id=1, replica_groups=mesh['fsdp'=8,'dp'=4] {'fsdp'}, dimensions={0}, use_global_device_ids=true | all-gather | bytes 6912 | tf_op jit(solution)/shard_map/all_gather | solution.py:115
  40.1 99.0 %all-gather.4.cloned.1.call-done = bf16[768,12288]{1,0:T(8,128)(2,1)} async-done(((bf16[24,12288]{1,0:T(8,128)(2,1)}), bf16[768,12288]{1,0:T(8,128)(2,1)}) %all-gather.4.cloned.1.call-update) | async-done | bytes 18874384 | tf_op jit(solution)/shard_map/all_gather | solution.py:64
  139.1 4.8 slice.124
  144.0 9.7 %reshape.392 = bf16[32,24,4,768]{3,2,1,0:T(4,128)(2,1)} reshape(bf16[768,3072]{1,0:T(8,128)(2,1)} %slice.124) | data formatting | bytes 9437184 | tf_op jit(solution)/shard_map/reshape | solution.py:67
  153.7 5.5 copy.108
  159.2 4.0 fusion.20
  163.2 1.5 copy-done.5
  164.7 2.4 copy.101
  167.1 4.2 reshape.390
  176.3 2.2 fusion.132
  179.1 8.3 %fusion.6 = f32[512,6144]{1,0:T(8,128)S(1)} fusion(bf16[512,768]{1,0:T(8,128)(2,1)S(1)} %fusion.49, bf16[768,12288]{1,0:T(8,128)(2,1)} %all-gather.4.cloned.1.call-done), kind=kOutput, calls=%fused_computation.9 | convolution fusion | flops 4831838208 | bytes 22806528 | tf_op jit(solution)/shard_map/dot_general | solution.py:16
  187.5 28.4 %fusion.133 = (f32[512]{0:T(512)}, f32[512,768]{1,0:T(8,128)S(1)}) fusion(bf16[3072,768]{1,0:T(8,128)(2,1)S(1)} %bitcast.158, f32[512,6144]{1,0:T(8,128)S(1)} %fusion.6, f32[768]{0:T(1024)S(1)} %get-tuple-element.20, f32[768]{0:T(1024)S(1)} %get-tuple-element.21, f32[512]{0:T(512)S(1)} %add_rsqrt_fusion.3, f32[512,768]{1,0:T(8,128)S(1)} %get-tuple-element.37, ...), kind=kOutput, calls=%fused_computation.229 | convolution fusion | flops 2522086912 | bytes 20459520 | tf_op jit(solution)/shard_map/dot_general | solution.py:16
  224.7 5.3 fusion.4
  230.0 5.1 fusion.32
  235.4 6.7 %multiply_reduce_fusion.4 = (f32[768]{0:T(1024)}, f32[128]{0:T(128)S(1)}, f32[128]{0:T(128)S(1)}, f32[768]{0:T(1024)}, f32[128,768]{1,0:T(8,128)S(1)}) fusion(f32[4,32,768]{2,1,0:T(8,128)S(1)} %get-tuple-element.43, f32[128]{0:T(128)S(1)} %div.77, f32[128]{0:T(128)S(1)} %rsqrt.42, f32[768]{0:T(1024)S(1)} %get-tuple-element.21, f32[128,768]{1,0:T(8,128)S(1)} %fusion.67, ...), kind=kOutput, calls=%fused_computation.116 | convolution fusion | flops 1212086528 | bytes 12200960 | tf_op jit(solution)/shard_map/nf,df->nd/dot_general | solution.py:161
  243.1 1.9 convolution_convert_fusion.7
  248.4 3.9 fusion.43
  252.3 2.0 multiply_reduce_fusion.2
  255.8 5.3 convolution_convert_fusion
  264.8 1.5 copy.118
  267.7 2.3 copy.119
  270.0 3.1 copy.132
  275.6 5.2 fusion.19
  280.8 4.3 copy.120
  285.1 15.7 %pad_maximum_fusion = bf16[768,12288]{1,0:T(8,128)(2,1)} fusion(bf16[768,3072]{1,0:T(8,128)(2,1)} %bitcast.149, bf16[768,6144]{1,0:T(8,128)(2,1)} %convolution_convert_fusion, bf16[768,768]{1,0:T(8,128)(2,1)} %copy.121, bf16[768,2304]{1,0:T(8,128)(2,1)S(1)} %copy.120), kind=kLoop, calls=%fused_computation.2 | loop fusion | flops 75497472 | bytes 37748736 | tf_op jit(solution)/shard_map/concatenate | solution.py:88
  300.9 205.2 %reduce-scatter.2.cloned.1.call-done = bf16[24,12288]{1,0:T(8,128)(2,1)} async-done(((bf16[768,12288]{1,0:T(8,128)(2,1)}), bf16[24,12288]{1,0:T(8,128)(2,1)}) %reduce-scatter.2.cloned.1.call-update) | async-done | bytes 589840 | tf_op jit(solution)/shard_map/reduce_scatter | solution.py:89
  509.4 40.4 %psum.7 = f32[4,768]{1,0:T(4,128)} all-reduce(f32[4,768]{1,0:T(4,128)} %pad_maximum_fusion.7), channel_id=1, replica_groups=mesh['fsdp'=8,'dp'=4] {'fsdp','dp'}, use_global_device_ids=true, to_apply=%region_22.23 | all-reduce | flops 3072 | bytes 24576 | tf_op jit(solution)/shard_map/psum | solution.py:202
  552.2 1.5 fusion.76
  555.0 5.2 bitcast_add_fusion
  560.2 2.3 slice.133
  562.5 1.9 reshape.413
  567.3 1.6 slice.132
  (170 shorter events, 47.7 us)
Async XLA Ops:
  7.2 132.0 %all-gather.4.cloned.1.call-start = ((), (), s32[]{:S(2)}) async-start(), calls=%async_computation.1 | async-start | bytes 19464192 | tf_op jit(solution)/shard_map/all_gather | solution.py:64
  12.2 493.8 %reduce-scatter.2.cloned.1.call-start = ((), (), s32[]{:S(2)}) async-start(), calls=%async_computation.2 | async-start | bytes 19464192 | tf_op jit(solution)/shard_map/reduce_scatter | solution.py:89
  38.4 180.8 %copy-start.28 = (pred[4,32]{1,0:T(4,128)(4,1)}, pred[4,32]{1,0:T(4,128)(4,1)S(1)}, u32[]{:S(2)}) copy-start(pred[4,32]{1,0:T(4,128)(4,1)S(1)} %get-tuple-element.33) | copy-start | bytes 388
  153.7 5.5 copy-start.36
  178.8 8.7 %slice-start = ((s8[4718592]{0:T(1024)(128)(4,1)}), s8[4194304]{0:T(1024)(128)(4,1)S(1)}, s32[]{:S(2)}) async-start(s8[4718592]{0:T(1024)(128)(4,1)} %bitcast.156), calls=%async_computation.4 | async-start | bytes 8388608
  179.1 8.3 %copy-start.10 = (bf16[512,768]{1,0:T(8,128)(2,1)}, bf16[512,768]{1,0:T(8,128)(2,1)S(1)}, u32[]{:S(2)}) copy-start(bf16[512,768]{1,0:T(8,128)(2,1)S(1)} %fusion.49) | copy-start | bytes 2359300
  179.1 8.4 %slice-start.1 = ((s8[4718592]{0:T(1024)(128)(4,1)}), s8[524288]{0:T(1024)(128)(4,1)S(1)}, s32[]{:S(2)}) async-start(s8[4718592]{0:T(1024)(128)(4,1)} %bitcast.156), calls=%async_computation.5 | async-start | bytes 1048576
  187.5 29.6 %copy-start.26 = (s32[4,32]{1,0:T(4,128)S(1)}, s32[4,32]{1,0:T(4,128)}, u32[]{:S(2)}) copy-start(s32[4,32]{1,0:T(4,128)} %param.22) | copy-start | bytes 1540
  187.5 31.7 %copy-start.12 = (bf16[4,32,768]{2,1,0:T(8,128)(2,1)S(1)}, bf16[4,32,768]{2,1,0:T(8,128)(2,1)}, u32[]{:S(2)}) copy-start(bf16[4,32,768]{2,1,0:T(8,128)(2,1)} %param.21) | copy-start | bytes 589828
  222.9 12.4 %copy-start.34 = (f32[128]{0:T(128)}, f32[128]{0:T(128)S(1)}, u32[]{:S(2)}) copy-start(f32[128]{0:T(128)S(1)} %div.77) | copy-start | bytes 1540
  223.2 12.2 %copy-start.35 = (f32[128]{0:T(128)}, f32[128]{0:T(128)S(1)}, u32[]{:S(2)}) copy-start(f32[128]{0:T(128)S(1)} %rsqrt.42) | copy-start | bytes 1540
  224.7 5.3 copy-start.20
  230.0 5.2 copy-start.29
  230.0 5.2 copy-start.30
  230.0 5.2 copy-start.31
  230.0 5.1 copy-start.32
  230.0 5.1 copy-start.33
  235.2 7.0 %copy-start.22 = (bf16[128,3072]{1,0:T(8,128)(2,1)}, bf16[128,3072]{1,0:T(8,128)(2,1)S(1)}, u32[]{:S(2)}) copy-start(bf16[128,3072]{1,0:T(8,128)(2,1)S(1)} %get-tuple-element.22) | copy-start | bytes 2359300
  235.2 7.0 %copy-start.24 = (bf16[128,3072]{1,0:T(8,128)(2,1)}, bf16[128,3072]{1,0:T(8,128)(2,1)S(1)}, u32[]{:S(2)}) copy-start(bf16[128,3072]{1,0:T(8,128)(2,1)S(1)} %get-tuple-element.23) | copy-start | bytes 2359300
  242.2 3.2 slice-start.2
  243.1 30.5 %copy-start.3 = (f32[128,768]{1,0:T(8,128)}, f32[128,768]{1,0:T(8,128)S(1)}, u32[]{:S(2)}) copy-start(f32[128,768]{1,0:T(8,128)S(1)} %subtract_multiply_fusion) | copy-start | bytes 1179652
  255.8 5.3 copy-start.19
  261.8 13.7 %copy-start.14 = (bf16[96,8,4,128]{3,1,2,0:T(8,128)(2,1)}, bf16[96,8,4,128]{3,1,2,0:T(8,128)(2,1)S(1)}, u32[]{:S(2)}) copy-start(bf16[96,8,4,128]{3,1,2,0:T(8,128)(2,1)S(1)} %copy.163) | copy-start | bytes 2359300
  262.6 13.0 %copy-start.16 = (bf16[96,8,4,128]{3,1,2,0:T(8,128)(2,1)}, bf16[96,8,4,128]{3,1,2,0:T(8,128)(2,1)S(1)}, u32[]{:S(2)}) copy-start(bf16[96,8,4,128]{3,1,2,0:T(8,128)(2,1)S(1)} %copy.164) | copy-start | bytes 2359300
  300.8 250.6 %copy-start.1 = (f32[512,768]{1,0:T(8,128)S(1)}, f32[512,768]{1,0:T(8,128)}, u32[]{:S(2)}) copy-start(f32[512,768]{1,0:T(8,128)} %copy-done) | copy-start | bytes 4718596
  300.8 251.4 %copy-start.4 = (f32[128,768]{1,0:T(8,128)S(1)}, f32[128,768]{1,0:T(8,128)}, u32[]{:S(2)}) copy-start(f32[128,768]{1,0:T(8,128)} %copy-done.3) | copy-start | bytes 1179652
  300.8 253.0 %copy-start.27 = (f32[768]{0:T(1024)S(1)}, f32[768]{0:T(1024)}, u32[]{:S(2)}) copy-start(f32[768]{0:T(1024)} %get-tuple-element.19) | copy-start | bytes 9220
  300.8 254.2 %copy-start.15 = (bf16[96,8,4,128]{3,1,2,0:T(8,128)(2,1)S(1)}, bf16[96,8,4,128]{3,1,2,0:T(8,128)(2,1)}, u32[]{:S(2)}) copy-start(bf16[96,8,4,128]{3,1,2,0:T(8,128)(2,1)} %copy-done.14) | copy-start | bytes 2359300
  300.8 254.2 %copy-start.17 = (bf16[96,8,4,128]{3,1,2,0:T(8,128)(2,1)S(1)}, bf16[96,8,4,128]{3,1,2,0:T(8,128)(2,1)}, u32[]{:S(2)}) copy-start(bf16[96,8,4,128]{3,1,2,0:T(8,128)(2,1)} %copy-done.16) | copy-start | bytes 2359300
  300.8 259.3 %all-gather.6.cloned.1.call-start = ((), (), s32[]{:S(2)}) async-start(), calls=%async_computation.3 | async-start | bytes 2949120 | tf_op jit(solution)/shard_map/all_gather | solution.py:90
  549.9 5.1 copy-start.18
  560.2 5.4 copy-start.2
  (12 other events, 21.4 us)
Sparse Core Ops, SparseCore 0:
  12.4 126.7 all-gather.3
  300.9 205.0 reduce-scatter.1
  507.6 23.6 all-gather.5
where the time goes:
time: 586 us; the launch traced here: 576 us
  waiting for transfers between devices  304 us (52%)
  matrix products  94.3 us (16%)
  local copies, waits for them, and re-layouts  68.5 us (12%)
  blocking collectives  63 us (11%)
  other arithmetic  30.7 us (5%)
  between operations  15 us (3%)
    reduce_scatter x1, waiting for transfers between devices, scatter_grads(): mine = lax.psum_scatter(joined, AXES, scatter_dimension=0, tiled=True)  205 us
    all_gather x1, waiting for transfers between devices, gather_weights(): lax.all_gather(jnp.concatenate([joined, down], axis=1), AXES, axis=0, til...  99 us
    dot_general x5, matrix products, mm(): return jnp.dot(a, b, preferred_element_type=F32)  48.2 us
    psum x1, blocking collectives, on_device(): lax.psum(jnp.stack([g_gain_attn, g_shift_attn, g_gain_ffn, g_shift_ffn]),...  40.4 us
    all_gather x1, blocking collectives, on_device(): norms = lax.all_gather(norms, 'fsdp', axis=1, tiled=True).astype(F32)  22.6 us
    concatenate x1, other arithmetic, scatter_grads(): joined = jnp.concatenate([g_qkv, g_out, g_up, down], axis=1).astype(LOW)  15.7 us
  transfers between devices with their start and end apart: 3, of which 2 were waited for; matrix products, arithmetic and copies ran while one was open for 3% of the time, Pallas kernels for 0%

commit v1 on v0

--- a/solution.py
+++ b/solution.py
@@ -2,6 +2,7 @@
 import jax.numpy as jnp
 from jax import lax
 from jax.sharding import PartitionSpec as P
+from jax.lax import all_to_all, axis_size
 
 HEADS = 12
 HEAD_DIM = 64
@@ -10,6 +11,11 @@
 F32 = jnp.float32
 LOW = jnp.bfloat16
 AXES = ("fsdp", "dp")
+
+
+def _press_series_all(dim_at, local):
+    val2 = jnp.concatenate([local for _ in range(axis_size("fsdp"))], axis=dim_at)
+    return all_to_all(val2, tiled=True, concat_axis=dim_at, axis_name="fsdp", split_axis=dim_at)
 
 
 def mm(a, b):
@@ -112,7 +118,7 @@
     tokens = seqs * length
     most = positions.shape[1]
     norms = jnp.stack([gain_attn, shift_attn, gain_ffn, shift_ffn])
-    norms = lax.all_gather(norms, "fsdp", axis=1, tiled=True).astype(F32)
+    norms = _press_series_all(1, norms).astype(F32)
     w_qkv, w_out, w_up, w_down = gather_weights(w_qkv, w_out, w_up, w_down)
     live = jnp.arange(most, dtype=jnp.int32)[None, :] < counts[:, None]
     onehot = (positions[:, :, None] == jnp.arange(length, dtype=jnp.int32)).astype(F32)

time: 586 us -> 587 us (level)
  blocking collectives: 63 us -> 40.3 us
  waiting for transfers between devices: 304 us -> 319 us
  starting transfers between devices: 0.12 us -> 7.43 us
    all_gather x1 -> x0, blocking collectives: 22.6 us -> none  [on_device(): norms = lax.all_gather(norms, 'fsdp', axis=1, tiled=True).astype(F32)]
    all_gather x1, waiting for transfers between devices: 99 us -> 111 us  [gather_weights(): lax.all_gather(jnp.concatenate([joined, down], axis=1), AXES, axis=0, til...]
    all_to_all x0 -> x1, starting transfers between devices: none -> 7.31 us  [_press_series_all(): all_to_all(val2, tiled=True, concat_axis=dim_at, axis_name='fsdp', split_...]
  transfers between devices with their start and end apart: 3 -> 4, of which waited for: 2 -> 3; matrix products, arithmetic and copies ran while one was open for 3% -> 4% of each run, Pallas kernels for 0% -> 0%
where the time goes in v1:
time: 587 us; the launch traced here: 576 us
  waiting for transfers between devices  319 us (54%)
  matrix products  94.3 us (16%)
  local copies, waits for them, and re-layouts  70.2 us (12%)
  blocking collectives  40.3 us (7%)
  other arithmetic  30.7 us (5%)
  between operations  15 us (3%)
  starting transfers between devices  7.43 us (1%)
    reduce_scatter x1, waiting for transfers between devices, scatter_grads(): mine = lax.psum_scatter(joined, AXES, scatter_dimension=0, tiled=True)  205 us
    all_gather x1, waiting for transfers between devices, gather_weights(): lax.all_gather(jnp.concatenate([joined, down], axis=1), AXES, axis=0, til...  111 us
    dot_general x5, matrix products, mm(): return jnp.dot(a, b, preferred_element_type=F32)  48.1 us
    psum x1, blocking collectives, on_device(): lax.psum(jnp.stack([g_gain_attn, g_shift_attn, g_gain_ffn, g_shift_ffn]),...  40.3 us
    concatenate x1, other arithmetic, scatter_grads(): joined = jnp.concatenate([g_qkv, g_out, g_up, down], axis=1).astype(LOW)  15.7 us
  transfers between devices with their start and end apart: 4, of which 3 were waited for; matrix products, arithmetic and copies ran while one was open for 4% of the time, Pallas kernels for 0%

profile of v1, /device:TPU:0, one launch (start us, length us, event | category | flops | bytes accessed | tf_op | source)
XLA Modules:
  0.0 576.4 jit_solution(15349918225113142681)
XLA Ops:
  13.8 7.3 %all-to-all-start = ((bf16[4,8,96]{2,0,1:T(4,128)(2,1)}), bf16[4,8,96]{2,0,1:T(4,128)(2,1)S(1)}, u32[]{:S(2)}, u32[]{:S(2)}) async-start(bf16[4,8,96]{2,0,1:T(4,128)(2,1)} %copy.83), calls=%async_computation | async-start | bytes 16384 | tf_op jit(solution)/shard_map/all_to_all | solution.py:18
  24.9 2.7 all-to-all-done
  28.4 110.6 %all-gather.3.cloned.1.call-done = bf16[768,12288]{1,0:T(8,128)(2,1)} async-done(((bf16[24,12288]{1,0:T(8,128)(2,1)}), bf16[768,12288]{1,0:T(8,128)(2,1)}) %all-gather.3.cloned.1.call-update) | async-done | bytes 18874384 | tf_op jit(solution)/shard_map/all_gather | solution.py:70
  139.1 4.8 slice.128
  143.9 9.7 %reshape.403 = bf16[32,24,4,768]{3,2,1,0:T(4,128)(2,1)} reshape(bf16[768,3072]{1,0:T(8,128)(2,1)} %slice.128) | data formatting | bytes 9437184 | tf_op jit(solution)/shard_map/reshape | solution.py:73
  153.6 5.5 copy.84
  159.1 4.0 fusion.20
  164.6 2.4 copy.77
  167.0 4.2 reshape.401
  176.2 2.2 fusion.132
  179.1 8.3 %fusion.6 = f32[512,6144]{1,0:T(8,128)S(1)} fusion(bf16[512,768]{1,0:T(8,128)(2,1)S(1)} %fusion.49, bf16[768,12288]{1,0:T(8,128)(2,1)} %all-gather.3.cloned.1.call-done), kind=kOutput, calls=%fused_computation.9 | convolution fusion | flops 4831838208 | bytes 22806528 | tf_op jit(solution)/shard_map/dot_general | solution.py:22
  187.5 28.4 %fusion.133 = (f32[512]{0:T(512)}, f32[512,768]{1,0:T(8,128)S(1)}) fusion(bf16[3072,768]{1,0:T(8,128)(2,1)S(1)} %bitcast.151, f32[512,6144]{1,0:T(8,128)S(1)} %fusion.6, f32[768]{0:T(1024)S(1)} %add.117, f32[768]{0:T(1024)S(1)} %mul.310, f32[512]{0:T(512)S(1)} %add_rsqrt_fusion.3, f32[512,768]{1,0:T(8,128)S(1)} %get-tuple-element.37, ...), kind=kOutput, calls=%fused_computation.228 | convolution fusion | flops 2522086912 | bytes 20459520 | tf_op jit(solution)/shard_map/dot_general | solution.py:22
  224.6 5.3 fusion.4
  230.0 5.1 fusion.32
  235.3 6.7 %multiply_reduce_fusion.4 = (f32[768]{0:T(1024)}, f32[128]{0:T(128)S(1)}, f32[128]{0:T(128)S(1)}, f32[768]{0:T(1024)}, f32[128,768]{1,0:T(8,128)S(1)}) fusion(f32[4,32,768]{2,1,0:T(8,128)S(1)} %get-tuple-element.43, f32[128]{0:T(128)S(1)} %div.77, f32[128]{0:T(128)S(1)} %rsqrt.42, f32[768]{0:T(1024)S(1)} %mul.310, f32[128,768]{1,0:T(8,128)S(1)} %fusion.67, ...), kind=kOutput, calls=%fused_computation.116 | convolution fusion | flops 1212086528 | bytes 12200960 | tf_op jit(solution)/shard_map/nf,df->nd/dot_general | solution.py:167
  243.0 1.9 convolution_convert_fusion.7
  248.3 3.9 fusion.43
  252.2 2.0 multiply_reduce_fusion.2
  255.7 5.3 convolution_convert_fusion
  264.7 1.5 copy.94
  267.6 2.3 copy.95
  270.0 3.1 copy.108
  275.5 5.2 fusion.19
  280.7 4.3 copy.96
  285.0 15.7 %pad_maximum_fusion = bf16[768,12288]{1,0:T(8,128)(2,1)} fusion(bf16[768,3072]{1,0:T(8,128)(2,1)} %bitcast.142, bf16[768,6144]{1,0:T(8,128)(2,1)} %convolution_convert_fusion, bf16[768,768]{1,0:T(8,128)(2,1)} %copy.97, bf16[768,2304]{1,0:T(8,128)(2,1)S(1)} %copy.96), kind=kLoop, calls=%fused_computation.2 | loop fusion | flops 75497472 | bytes 37748736 | tf_op jit(solution)/shard_map/concatenate | solution.py:94
  300.8 205.2 %reduce-scatter.2.cloned.1.call-done = bf16[24,12288]{1,0:T(8,128)(2,1)} async-done(((bf16[768,12288]{1,0:T(8,128)(2,1)}), bf16[24,12288]{1,0:T(8,128)(2,1)}) %reduce-scatter.2.cloned.1.call-update) | async-done | bytes 589840 | tf_op jit(solution)/shard_map/reduce_scatter | solution.py:95
  510.0 40.3 %psum.7 = f32[4,768]{1,0:T(4,128)} all-reduce(f32[4,768]{1,0:T(4,128)} %pad_maximum_fusion.7), channel_id=1, replica_groups=mesh['fsdp'=8,'dp'=4] {'fsdp','dp'}, use_global_device_ids=true, to_apply=%region_22.23 | all-reduce | flops 3072 | bytes 24576 | tf_op jit(solution)/shard_map/psum | solution.py:208
  552.7 1.6 fusion.76
  555.5 5.2 bitcast_add_fusion
  560.7 2.3 slice.137
  563.0 1.9 reshape.424
  567.8 1.6 slice.136
  (179 shorter events, 50.8 us)
Async XLA Ops:
  7.2 131.9 %all-gather.3.cloned.1.call-start = ((), (), s32[]{:S(2)}) async-start(), calls=%async_computation.2 | async-start | bytes 19464192 | tf_op jit(solution)/shard_map/all_gather | solution.py:70
  13.8 13.8 %all-to-all-start = ((bf16[4,8,96]{2,0,1:T(4,128)(2,1)}), bf16[4,8,96]{2,0,1:T(4,128)(2,1)S(1)}, u32[]{:S(2)}, u32[]{:S(2)}) async-start(bf16[4,8,96]{2,0,1:T(4,128)(2,1)} %copy.83), calls=%async_computation | async-start | bytes 16384 | tf_op jit(solution)/shard_map/all_to_all | solution.py:18
  21.1 484.9 %reduce-scatter.2.cloned.1.call-start = ((), (), s32[]{:S(2)}) async-start(), calls=%async_computation.3 | async-start | bytes 19464192 | tf_op jit(solution)/shard_map/reduce_scatter | solution.py:95
  22.6 196.6 %copy-start.29 = (pred[4,32]{1,0:T(4,128)(4,1)}, pred[4,32]{1,0:T(4,128)(4,1)S(1)}, u32[]{:S(2)}) copy-start(pred[4,32]{1,0:T(4,128)(4,1)S(1)} %get-tuple-element.33) | copy-start | bytes 388
  153.6 5.5 copy-start.37
  178.7 8.7 %slice-start = ((s8[4718592]{0:T(1024)(128)(4,1)}), s8[4194304]{0:T(1024)(128)(4,1)S(1)}, s32[]{:S(2)}) async-start(s8[4718592]{0:T(1024)(128)(4,1)} %bitcast.149), calls=%async_computation.5 | async-start | bytes 8388608
  179.0 8.3 %copy-start.10 = (bf16[512,768]{1,0:T(8,128)(2,1)}, bf16[512,768]{1,0:T(8,128)(2,1)S(1)}, u32[]{:S(2)}) copy-start(bf16[512,768]{1,0:T(8,128)(2,1)S(1)} %fusion.49) | copy-start | bytes 2359300
  179.1 8.4 %slice-start.1 = ((s8[4718592]{0:T(1024)(128)(4,1)}), s8[524288]{0:T(1024)(128)(4,1)S(1)}, s32[]{:S(2)}) async-start(s8[4718592]{0:T(1024)(128)(4,1)} %bitcast.149), calls=%async_computation.6 | async-start | bytes 1048576
  187.4 29.6 %copy-start.26 = (s32[4,32]{1,0:T(4,128)S(1)}, s32[4,32]{1,0:T(4,128)}, u32[]{:S(2)}) copy-start(s32[4,32]{1,0:T(4,128)} %param.22) | copy-start | bytes 1540
  187.4 31.7 %copy-start.12 = (bf16[4,32,768]{2,1,0:T(8,128)(2,1)S(1)}, bf16[4,32,768]{2,1,0:T(8,128)(2,1)}, u32[]{:S(2)}) copy-start(bf16[4,32,768]{2,1,0:T(8,128)(2,1)} %param.21) | copy-start | bytes 589828
  222.9 12.4 %copy-start.35 = (f32[128]{0:T(128)}, f32[128]{0:T(128)S(1)}, u32[]{:S(2)}) copy-start(f32[128]{0:T(128)S(1)} %div.77) | copy-start | bytes 1540
  223.2 12.2 %copy-start.36 = (f32[128]{0:T(128)}, f32[128]{0:T(128)S(1)}, u32[]{:S(2)}) copy-start(f32[128]{0:T(128)S(1)} %rsqrt.42) | copy-start | bytes 1540
  224.6 5.3 copy-start.20
  229.9 5.2 copy-start.30
  229.9 5.2 copy-start.31
  229.9 5.2 copy-start.32
  229.9 5.1 copy-start.33
  229.9 5.1 copy-start.34
  235.1 7.0 %copy-start.22 = (bf16[128,3072]{1,0:T(8,128)(2,1)}, bf16[128,3072]{1,0:T(8,128)(2,1)S(1)}, u32[]{:S(2)}) copy-start(bf16[128,3072]{1,0:T(8,128)(2,1)S(1)} %get-tuple-element.22) | copy-start | bytes 2359300
  235.1 7.0 %copy-start.24 = (bf16[128,3072]{1,0:T(8,128)(2,1)}, bf16[128,3072]{1,0:T(8,128)(2,1)S(1)}, u32[]{:S(2)}) copy-start(bf16[128,3072]{1,0:T(8,128)(2,1)S(1)} %get-tuple-element.23) | copy-start | bytes 2359300
  243.0 30.5 %copy-start.3 = (f32[128,768]{1,0:T(8,128)}, f32[128,768]{1,0:T(8,128)S(1)}, u32[]{:S(2)}) copy-start(f32[128,768]{1,0:T(8,128)S(1)} %subtract_multiply_fusion) | copy-start | bytes 1179652
  255.7 5.3 copy-start.19
  261.8 13.7 %copy-start.14 = (bf16[96,8,4,128]{3,1,2,0:T(8,128)(2,1)}, bf16[96,8,4,128]{3,1,2,0:T(8,128)(2,1)S(1)}, u32[]{:S(2)}) copy-start(bf16[96,8,4,128]{3,1,2,0:T(8,128)(2,1)S(1)} %copy.138) | copy-start | bytes 2359300
  262.5 13.0 %copy-start.16 = (bf16[96,8,4,128]{3,1,2,0:T(8,128)(2,1)}, bf16[96,8,4,128]{3,1,2,0:T(8,128)(2,1)S(1)}, u32[]{:S(2)}) copy-start(bf16[96,8,4,128]{3,1,2,0:T(8,128)(2,1)S(1)} %copy.139) | copy-start | bytes 2359300
  300.7 207.3 %copy-start.27 = (f32[768]{0:T(1024)S(1)}, f32[768]{0:T(1024)}, u32[]{:S(2)}) copy-start(f32[768]{0:T(1024)} %get-tuple-element.12) | copy-start | bytes 9220
  300.7 251.2 %copy-start.1 = (f32[512,768]{1,0:T(8,128)S(1)}, f32[512,768]{1,0:T(8,128)}, u32[]{:S(2)}) copy-start(f32[512,768]{1,0:T(8,128)} %copy-done) | copy-start | bytes 4718596
  300.7 252.0 %copy-start.4 = (f32[128,768]{1,0:T(8,128)S(1)}, f32[128,768]{1,0:T(8,128)}, u32[]{:S(2)}) copy-start(f32[128,768]{1,0:T(8,128)} %copy-done.3) | copy-start | bytes 1179652
  300.7 254.8 %copy-start.15 = (bf16[96,8,4,128]{3,1,2,0:T(8,128)(2,1)S(1)}, bf16[96,8,4,128]{3,1,2,0:T(8,128)(2,1)}, u32[]{:S(2)}) copy-start(bf16[96,8,4,128]{3,1,2,0:T(8,128)(2,1)} %copy-done.14) | copy-start | bytes 2359300
  300.7 254.8 %copy-start.17 = (bf16[96,8,4,128]{3,1,2,0:T(8,128)(2,1)S(1)}, bf16[96,8,4,128]{3,1,2,0:T(8,128)(2,1)}, u32[]{:S(2)}) copy-start(bf16[96,8,4,128]{3,1,2,0:T(8,128)(2,1)} %copy-done.16) | copy-start | bytes 2359300
  300.8 259.9 %all-gather.5.cloned.1.call-start = ((), (), s32[]{:S(2)}) async-start(), calls=%async_computation.4 | async-start | bytes 2949120 | tf_op jit(solution)/shard_map/all_gather | solution.py:96
  508.0 46.2 %copy-start.28 = (f32[768]{0:T(1024)S(1)}, f32[768]{0:T(1024)}, u32[]{:S(2)}) copy-start(f32[768]{0:T(1024)} %add.122) | copy-start | bytes 9220
  560.7 5.4 copy-start.2
  (14 other events, 29.7 us)
Sparse Core Ops, SparseCore 0:
  12.4 126.6 all-gather.2
  300.9 205.0 reduce-scatter.1
  507.5 23.8 all-gather.4
